TPU v7x, 32 devices: a whole 2x2x4 slice. The times are simulated.
32 devices in a mesh: seq: 4 (over z), fsdp: 8 (over y, x, core).
Axes of the slice: x: 2, y: 2, z: 4, core: 2. Of those that a mesh axis runs over, the one named last changes fastest.
Arguments:
- inputs: bfloat16 [8, 1024, 2048], P('fsdp', 'seq'), may hold values from -6 to 6
- norm1_gain: bfloat16 [2048], P(('seq', 'fsdp')), may hold values from 0.5 to 1.5
- w_query: bfloat16 [2048, 2048], P(('seq', 'fsdp')), may hold values from -0.125 to 0.125
- w_key: bfloat16 [2048, 2048], P(('seq', 'fsdp')), may hold values from -0.125 to 0.125
- w_value: bfloat16 [2048, 2048], P(('seq', 'fsdp')), may hold values from -0.125 to 0.125
- w_output: bfloat16 [2048, 2048], P(('seq', 'fsdp')), may hold values from -0.5 to 0.5
- norm2_gain: bfloat16 [2048], P(('seq', 'fsdp')), may hold values from 0.5 to 1.5
- w_gate: bfloat16 [2048, 8192], P(('seq', 'fsdp')), may hold values from -0.125 to 0.125
- w_up: bfloat16 [2048, 8192], P(('seq', 'fsdp')), may hold values from -0.125 to 0.125
- w_down: bfloat16 [8192, 2048], P(('seq', 'fsdp')), may hold values from -0.0625 to 0.0625
- out_grad: bfloat16 [8, 1024, 2048], P('fsdp', 'seq'), may hold values from -6 to 6
Outputs:
- output: bfloat16 [8, 1024, 2048], P('fsdp', 'seq')
- input_grad: float32 [8, 1024, 2048], P('fsdp', 'seq')
- norm1_gain_grad: float32 [2048], P(('seq', 'fsdp'))
- w_query_grad: float32 [2048, 2048], P(('seq', 'fsdp'))
- w_key_grad: float32 [2048, 2048], P(('seq', 'fsdp'))
- w_value_grad: float32 [2048, 2048], P(('seq', 'fsdp'))
- w_output_grad: float32 [2048, 2048], P(('seq', 'fsdp'))
- norm2_gain_grad: float32 [2048], P(('seq', 'fsdp'))
- w_gate_grad: float32 [2048, 8192], P(('seq', 'fsdp'))
- w_up_grad: float32 [2048, 8192], P(('seq', 'fsdp'))
- w_down_grad: float32 [8192, 2048], P(('seq', 'fsdp'))
All inputs are finite; a program needn't handle non-finite values.
Results may differ from a plain program's by a relative error of at most 0.014.
Values may be sent and summed in bfloat16 or wider, within the bound.
No kernel may reach another device: no remote copies, remote signals or barrier semaphores. Data moves between devices by JAX's collectives and lax.ppermute only.
A program may use at most 576 MiB of HBM per device.

v0:
```python
import math
import jax
import jax.numpy as jnp
from jax import lax
from jax.sharding import PartitionSpec as P

HEAD_DIM = 64
QBLK = 512
EPS = 1e-05
ROPE_BASE = 130000.0
NEG_FILL = -1e30


def tables(positions):
    half_dim = HEAD_DIM // 2
    freqs = jnp.exp(
        jnp.arange(half_dim, dtype=jnp.float32) * (-2.0 * math.log(ROPE_BASE) / HEAD_DIM)
    )
    angle = positions.astype(jnp.float32)[:, None] * freqs[None, :]
    angle = jnp.concatenate([angle, angle], axis=1)
    return (jnp.cos(angle), jnp.sin(angle))


def rotate_half(values):
    half_dim = values.shape[-1] // 2
    return jnp.concatenate([-values[..., half_dim:], values[..., :half_dim]], axis=-1)


def rotary(values, cosine, sine):
    seq_count, local_len, model_width = values.shape
    shaped = values.reshape(seq_count, local_len, model_width // HEAD_DIM, HEAD_DIM)
    turned = shaped * cosine[None, :, None, :] + rotate_half(shaped) * sine[None, :, None, :]
    return turned.reshape(seq_count, local_len, model_width)


def rotary_back(grads, cosine, sine):
    seq_count, local_len, model_width = grads.shape
    shaped = grads.reshape(seq_count, local_len, model_width // HEAD_DIM, HEAD_DIM)
    turned = shaped * cosine[None, :, None, :] - rotate_half(shaped * sine[None, :, None, :])
    return turned.reshape(seq_count, local_len, model_width)


def matmul(left, right):
    return jnp.dot(left, right, preferred_element_type=jnp.float32)


def outer_sum(left, right):
    return lax.dot_general(
        left, right, (((0,), (0,)), ((), ())), preferred_element_type=jnp.float32
    )


def times_transposed(left, right):
    return lax.dot_general(
        left, right, (((1,), (1,)), ((), ())), preferred_element_type=jnp.float32
    )


def normalize(values, gain):
    inverse = lax.rsqrt(jnp.mean(values * values, axis=1, keepdims=True) + EPS)
    return ((values * inverse * gain).astype(jnp.bfloat16), inverse)


def norm_back(grad_normed, values, inverse, gain):
    scaled = grad_normed * gain
    gain_term = jnp.sum(grad_normed * values * inverse, axis=0)
    value_grad = inverse * (
        scaled - values * inverse * inverse * jnp.mean(scaled * values, axis=1, keepdims=True)
    )
    return (gain_term, value_grad)


def causal_block(query_block, key_heads, block_start):
    score_scale = HEAD_DIM ** (-0.5)
    scores = (
        jnp.einsum("sqhd,skhd->shqk", query_block, key_heads, preferred_element_type=jnp.float32)
        * score_scale
    )
    query_pos = block_start + jnp.arange(query_block.shape[1])
    allowed = jnp.arange(key_heads.shape[1])[None, :] <= query_pos[:, None]
    return jnp.where(allowed, scores, NEG_FILL)


def local(
    inputs,
    norm1_gain,
    w_query,
    w_key,
    w_value,
    w_output,
    norm2_gain,
    w_gate,
    w_up,
    w_down,
    out_grad,
):
    seq_count, local_len, model_width = inputs.shape
    row_count = seq_count * local_len
    score_scale = HEAD_DIM ** (-0.5)
    residual_in = inputs.reshape(row_count, model_width).astype(jnp.float32)
    attn_set = (
        lax.all_gather(norm1_gain, ("seq", "fsdp"), axis=0, tiled=True),
        lax.all_gather(w_query, ("seq", "fsdp"), axis=0, tiled=True),
        lax.all_gather(w_key, ("seq", "fsdp"), axis=0, tiled=True),
        lax.all_gather(w_value, ("seq", "fsdp"), axis=0, tiled=True),
        lax.all_gather(w_output, ("seq", "fsdp"), axis=0, tiled=True),
    )
    gain_one, query_w, key_w, value_w, output_w = attn_set
    normed_one, inverse_one = normalize(residual_in, gain_one.astype(jnp.float32))
    positions = lax.axis_index("seq") * local_len + jnp.arange(local_len, dtype=jnp.int32)
    cosine, sine = tables(positions)
    query_rot = rotary(
        matmul(normed_one, query_w).reshape(seq_count, local_len, model_width), cosine, sine
    ).astype(jnp.bfloat16)
    key_rot = rotary(
        matmul(normed_one, key_w).reshape(seq_count, local_len, model_width), cosine, sine
    ).astype(jnp.bfloat16)
    value_tok = (
        matmul(normed_one, value_w).astype(jnp.bfloat16).reshape(seq_count, local_len, model_width)
    )
    query_h, key_h, value_h = (
        lax.all_to_all(query_rot, "seq", split_axis=2, concat_axis=1, tiled=True),
        lax.all_to_all(key_rot, "seq", split_axis=2, concat_axis=1, tiled=True),
        lax.all_to_all(value_tok, "seq", split_axis=2, concat_axis=1, tiled=True),
    )
    full_len = query_h.shape[1]
    head_width = query_h.shape[2]
    heads_here = head_width // HEAD_DIM
    query_heads = query_h.reshape(seq_count, full_len, heads_here, HEAD_DIM)
    key_heads = key_h.reshape(seq_count, full_len, heads_here, HEAD_DIM)
    value_heads = value_h.reshape(seq_count, full_len, heads_here, HEAD_DIM)
    block_outs = []
    block_lse = []
    for block_start in range(0, full_len, QBLK):
        block_end = block_start + QBLK
        query_block = query_heads[:, block_start:block_end]
        scores = causal_block(query_block, key_heads[:, :block_end], block_start)
        row_max = jnp.max(scores, axis=-1, keepdims=True)
        shifted = jnp.exp(scores - row_max)
        row_sum = jnp.sum(shifted, axis=-1, keepdims=True)
        attn_prob = (shifted / row_sum).astype(jnp.bfloat16)
        block_outs.append(
            jnp.einsum(
                "shqk,skhd->sqhd",
                attn_prob,
                value_heads[:, :block_end],
                preferred_element_type=jnp.float32,
            )
        )
        block_lse.append(row_max + jnp.log(row_sum))
    attended = (
        jnp.concatenate(block_outs, axis=1)
        .astype(jnp.bfloat16)
        .reshape(seq_count, full_len, head_width)
    )
    attended_tok = lax.all_to_all(attended, "seq", split_axis=1, concat_axis=2, tiled=True).reshape(
        row_count, model_width
    )
    mid_stream = residual_in + matmul(attended_tok, output_w)
    gain_two, gate_w, up_w, down_w = (
        lax.all_gather(norm2_gain, ("seq", "fsdp"), axis=0, tiled=True),
        lax.all_gather(w_gate, ("seq", "fsdp"), axis=0, tiled=True),
        lax.all_gather(w_up, ("seq", "fsdp"), axis=0, tiled=True),
        lax.all_gather(w_down, ("seq", "fsdp"), axis=0, tiled=True),
    )
    normed_two, inverse_two = normalize(mid_stream, gain_two.astype(jnp.float32))
    gate_pre = matmul(normed_two, gate_w)
    up_pre = matmul(normed_two, up_w)
    gate_sig = jax.nn.sigmoid(gate_pre)
    hidden = (gate_pre * gate_sig * up_pre).astype(jnp.bfloat16)
    output = (
        (mid_stream + matmul(hidden, down_w))
        .astype(jnp.bfloat16)
        .reshape(seq_count, local_len, model_width)
    )
    grad_out = out_grad.reshape(row_count, model_width).astype(jnp.float32)
    grad_outb = grad_out.astype(jnp.bfloat16)
    down_grad = lax.psum_scatter(
        outer_sum(hidden, grad_outb), ("seq", "fsdp"), scatter_dimension=0, tiled=True
    )
    gain_two, gate_w, up_w, down_w = (
        lax.all_gather(norm2_gain, ("seq", "fsdp"), axis=0, tiled=True),
        lax.all_gather(w_gate, ("seq", "fsdp"), axis=0, tiled=True),
        lax.all_gather(w_up, ("seq", "fsdp"), axis=0, tiled=True),
        lax.all_gather(w_down, ("seq", "fsdp"), axis=0, tiled=True),
    )
    grad_hidden = times_transposed(grad_outb, down_w)
    grad_gate = (grad_hidden * up_pre * gate_sig * (1.0 + gate_pre * (1.0 - gate_sig))).astype(
        jnp.bfloat16
    )
    grad_up = (grad_hidden * gate_pre * gate_sig).astype(jnp.bfloat16)
    grad_normed_two = times_transposed(grad_gate, gate_w) + times_transposed(grad_up, up_w)
    gain_two_term, grad_mid = norm_back(
        grad_normed_two, mid_stream, inverse_two, gain_two.astype(jnp.float32)
    )
    grad_mid = grad_out + grad_mid
    gate_grad, gain_two_grad = (
        lax.psum_scatter(
            outer_sum(normed_two, grad_gate), ("seq", "fsdp"), scatter_dimension=0, tiled=True
        ),
        lax.psum_scatter(gain_two_term, ("seq", "fsdp"), scatter_dimension=0, tiled=True),
    )
    up_grad = lax.psum_scatter(
        outer_sum(normed_two, grad_up), ("seq", "fsdp"), scatter_dimension=0, tiled=True
    )
    gain_one, query_w, key_w, value_w, output_w = (
        lax.all_gather(norm1_gain, ("seq", "fsdp"), axis=0, tiled=True),
        lax.all_gather(w_query, ("seq", "fsdp"), axis=0, tiled=True),
        lax.all_gather(w_key, ("seq", "fsdp"), axis=0, tiled=True),
        lax.all_gather(w_value, ("seq", "fsdp"), axis=0, tiled=True),
        lax.all_gather(w_output, ("seq", "fsdp"), axis=0, tiled=True),
    )
    grad_proj = grad_mid.astype(jnp.bfloat16)
    output_term = outer_sum(attended_tok, grad_proj)
    grad_att = (
        times_transposed(grad_proj, output_w)
        .astype(jnp.bfloat16)
        .reshape(seq_count, local_len, model_width)
    )
    grad_att_h = lax.all_to_all(grad_att, "seq", split_axis=2, concat_axis=1, tiled=True)
    grad_heads = grad_att_h.reshape(seq_count, full_len, heads_here, HEAD_DIM)
    grad_key_sum = jnp.zeros(key_heads.shape, jnp.float32)
    grad_value_sum = jnp.zeros(value_heads.shape, jnp.float32)
    query_parts = []
    for block_index, block_start in enumerate(range(0, full_len, QBLK)):
        block_end = block_start + QBLK
        query_block = query_heads[:, block_start:block_end]
        grad_block = grad_heads[:, block_start:block_end]
        key_part = key_heads[:, :block_end]
        value_part = value_heads[:, :block_end]
        scores = causal_block(query_block, key_part, block_start)
        attn_prob = jnp.exp(scores - block_lse[block_index])
        grad_prob = jnp.einsum(
            "sqhd,skhd->shqk", grad_block, value_part, preferred_element_type=jnp.float32
        )
        row_dot = jnp.sum(attn_prob * grad_prob, axis=-1, keepdims=True)
        grad_score = (attn_prob * (grad_prob - row_dot)).astype(jnp.bfloat16)
        query_parts.append(
            jnp.einsum("shqk,skhd->sqhd", grad_score, key_part, preferred_element_type=jnp.float32)
            * score_scale
        )
        grad_key_sum = grad_key_sum.at[:, :block_end].add(
            jnp.einsum(
                "shqk,sqhd->skhd", grad_score, query_block, preferred_element_type=jnp.float32
            )
            * score_scale
        )
        grad_value_sum = grad_value_sum.at[:, :block_end].add(
            jnp.einsum(
                "shqk,sqhd->skhd",
                attn_prob.astype(jnp.bfloat16),
                grad_block,
                preferred_element_type=jnp.float32,
            )
        )
    grad_query_h = (
        jnp.concatenate(query_parts, axis=1)
        .astype(jnp.bfloat16)
        .reshape(seq_count, full_len, head_width)
    )
    grad_key_h = grad_key_sum.astype(jnp.bfloat16).reshape(seq_count, full_len, head_width)
    grad_value_h = grad_value_sum.astype(jnp.bfloat16).reshape(seq_count, full_len, head_width)
    grad_query_t, grad_key_t, grad_value_t = (
        lax.all_to_all(grad_query_h, "seq", split_axis=1, concat_axis=2, tiled=True),
        lax.all_to_all(grad_key_h, "seq", split_axis=1, concat_axis=2, tiled=True),
        lax.all_to_all(grad_value_h, "seq", split_axis=1, concat_axis=2, tiled=True),
    )
    grad_query = (
        rotary_back(grad_query_t.astype(jnp.float32), cosine, sine)
        .astype(jnp.bfloat16)
        .reshape(row_count, model_width)
    )
    grad_key = (
        rotary_back(grad_key_t.astype(jnp.float32), cosine, sine)
        .astype(jnp.bfloat16)
        .reshape(row_count, model_width)
    )
    grad_value = grad_value_t.reshape(row_count, model_width)
    grad_normed_one = (
        times_transposed(grad_query, query_w)
        + times_transposed(grad_key, key_w)
        + times_transposed(grad_value, value_w)
    )
    gain_one_term, grad_in = norm_back(
        grad_normed_one, residual_in, inverse_one, gain_one.astype(jnp.float32)
    )
    input_grad = (grad_mid + grad_in).reshape(seq_count, local_len, model_width)
    query_grad, key_grad, value_grad, output_grad, gain_one_grad = (
        lax.psum_scatter(
            outer_sum(normed_one, grad_query), ("seq", "fsdp"), scatter_dimension=0, tiled=True
        ),
        lax.psum_scatter(
            outer_sum(normed_one, grad_key), ("seq", "fsdp"), scatter_dimension=0, tiled=True
        ),
        lax.psum_scatter(
            outer_sum(normed_one, grad_value), ("seq", "fsdp"), scatter_dimension=0, tiled=True
        ),
        lax.psum_scatter(output_term, ("seq", "fsdp"), scatter_dimension=0, tiled=True),
        lax.psum_scatter(gain_one_term, ("seq", "fsdp"), scatter_dimension=0, tiled=True),
    )
    return (
        output,
        input_grad,
        gain_one_grad,
        query_grad,
        key_grad,
        value_grad,
        output_grad,
        gain_two_grad,
        gate_grad,
        up_grad,
        down_grad,
    )


def solution(mesh):
    in_specs = (
        P("fsdp", "seq", None),
        P(("seq", "fsdp")),
        P(("seq", "fsdp"), None),
        P(("seq", "fsdp"), None),
        P(("seq", "fsdp"), None),
        P(("seq", "fsdp"), None),
        P(("seq", "fsdp")),
        P(("seq", "fsdp"), None),
        P(("seq", "fsdp"), None),
        P(("seq", "fsdp"), None),
        P("fsdp", "seq", None),
    )
    out_specs = (
        P("fsdp", "seq", None),
        P("fsdp", "seq", None),
        P(("seq", "fsdp")),
        P(("seq", "fsdp"), None),
        P(("seq", "fsdp"), None),
        P(("seq", "fsdp"), None),
        P(("seq", "fsdp"), None),
        P(("seq", "fsdp")),
        P(("seq", "fsdp"), None),
        P(("seq", "fsdp"), None),
        P(("seq", "fsdp"), None),
    )
    return jax.shard_map(local, mesh=mesh, in_specs=in_specs, out_specs=out_specs, check_vma=False)
```

profile of v0, /device:TPU:14, one launch (start us, length us, event | category | flops | bytes accessed | tf_op | source)
XLA Modules:
  0.0 3977.1 jit_solution(12633569938991020945)
XLA Ops:
  12.4 40.6 %all-reduce.7 = (bf16[2048]{0:T(1024)(128)(2,1)S(1)}, bf16[2048]{0:T(1024)(128)(2,1)S(1)}) all-reduce(bf16[2048]{0:T(1024)(128)(2,1)S(1)} %dynamic-update-slice.10, bf16[2048]{0:T(1024)(128)(2,1)S(1)} %dynamic-update-slice.11), channel_id=1, replica_groups=mesh['seq'=4,'fsdp'=8] {'seq','fsdp'}, use_global_device_ids=true, to_apply=%add.2 | all-reduce | flops 4096 | bytes 16384
  60.9 28.0 all-gather.8.cloned.1.call-done
  117.1 66.3 %all-gather.12.cloned.1.call-done = bf16[2048,2048]{1,0:T(8,128)(2,1)} async-done(((bf16[64,2048]{1,0:T(8,128)(2,1)}), bf16[2048,2048]{1,0:T(8,128)(2,1)}) %all-gather.12.cloned.1.call-update) | async-done | bytes 8388624 | tf_op jit(solution)/shard_map/all_gather | solution.py:104
  193.4 69.0 %all-gather.10.cloned.1.call-done = bf16[2048,2048]{1,0:T(8,128)(2,1)} async-done(((bf16[64,2048]{1,0:T(8,128)(2,1)}), bf16[2048,2048]{1,0:T(8,128)(2,1)}) %all-gather.10.cloned.1.call-update) | async-done | bytes 8388624 | tf_op jit(solution)/shard_map/all_gather | solution.py:103
  327.6 28.2 all-to-all-done.2
  382.0 20.6 all-to-all-done.1
  463.2 44.9 %all-to-all-done.3 = bf16[4,2,65536]{2,1,0:T(2,128)(2,1)S(1)} async-done(((bf16[4,2,65536]{2,1,0:T(2,128)(2,1)}), bf16[4,2,65536]{2,1,0:T(2,128)(2,1)S(1)}, u32[]{:S(2)}, u32[]{:S(2)}) %all-to-all-start.3) | async-done | bytes 1048608 | tf_op jit(solution)/shard_map/all_to_all | solution.py:156
  520.5 56.0 %all-gather.18.cloned.1.call-done = bf16[2048,8192]{1,0:T(8,128)(2,1)} async-done(((bf16[64,8192]{1,0:T(8,128)(2,1)}), bf16[2048,8192]{1,0:T(8,128)(2,1)}) %all-gather.18.cloned.1.call-update) | async-done | bytes 33554448 | tf_op jit(solution)/shard_map/all_gather | solution.py:163
  593.7 183.1 %all-gather.16.cloned.1.call-done = bf16[2048,8192]{1,0:T(8,128)(2,1)} async-done(((bf16[64,8192]{1,0:T(8,128)(2,1)}), bf16[2048,8192]{1,0:T(8,128)(2,1)}) %all-gather.16.cloned.1.call-update) | async-done | bytes 33554448 | tf_op jit(solution)/shard_map/all_gather | solution.py:162
  793.9 178.7 %all-gather.20.cloned.1.call-done = bf16[8192,2048]{1,0:T(8,128)(2,1)} async-done(((bf16[256,2048]{1,0:T(8,128)(2,1)}), bf16[8192,2048]{1,0:T(8,128)(2,1)}) %all-gather.20.cloned.1.call-update) | async-done | bytes 33554448 | tf_op jit(solution)/shard_map/all_gather | solution.py:164
  972.6 24.4 multiply_convert_fusion.2
  1070.5 28.8 all-to-all-done.4
  1131.6 58.2 %all_to_all.108 = bf16[4,2,65536]{2,1,0:T(2,128)(2,1)S(1)} all-to-all(bf16[4,2,65536]{2,1,0:T(2,128)(2,1)} %reshape.887), channel_id=1, replica_groups=mesh['seq'=4,'fsdp'=8] {'seq'}, dimensions={0} | all-to-all | bytes 2097152 | tf_op jit(solution)/shard_map/all_to_all | solution.py:266
  1316.0 17.4 all-to-all-done.6
  1368.1 26.2 fusion.52
  1395.5 26.3 fusion.83
  1421.9 26.2 fusion.82
  1449.7 17.6 fusion.22
  1486.0 53.6 %all-reduce.6 = (f32[2048]{0:T(1024)S(1)}, f32[2048]{0:T(1024)S(1)}) all-reduce(f32[2048]{0:T(1024)S(1)} %get-tuple-element.77, f32[2048]{0:T(1024)S(1)} %copy-done.48), channel_id=2, replica_groups=mesh['seq'=4,'fsdp'=8] {'seq','fsdp'}, use_global_device_ids=true, to_apply=%region_11.12.clone | all-reduce | flops 4096 | bytes 32768
  1544.4 100.8 %reduce-scatter.8.cloned.1.call-done = f32[64,2048]{1,0:T(8,128)} async-done(((f32[2048,2048]{1,0:T(8,128)}), f32[64,2048]{1,0:T(8,128)}) %reduce-scatter.8.cloned.1.call-update) | async-done | bytes 524304 | tf_op jit(solution)/shard_map/reduce_scatter | solution.py:289
  1645.1 187.4 %reduce-scatter.10.cloned.1.call-done = f32[64,2048]{1,0:T(8,128)} async-done(((f32[2048,2048]{1,0:T(8,128)}), f32[64,2048]{1,0:T(8,128)}) %reduce-scatter.10.cloned.1.call-update) | async-done | bytes 524304 | tf_op jit(solution)/shard_map/reduce_scatter | solution.py:292
  1832.5 711.7 %reduce-scatter.20.cloned.1.call-done = f32[256,2048]{1,0:T(8,128)} async-done(((f32[8192,2048]{1,0:T(8,128)}), f32[256,2048]{1,0:T(8,128)}) %reduce-scatter.20.cloned.1.call-update) | async-done | bytes 2097168 | tf_op jit(solution)/shard_map/reduce_scatter | solution.py:178
  2544.2 713.2 %reduce-scatter.18.cloned.1.call-done = f32[64,8192]{1,0:T(8,128)} async-done(((f32[2048,8192]{1,0:T(8,128)}), f32[64,8192]{1,0:T(8,128)}) %reduce-scatter.18.cloned.1.call-update) | async-done | bytes 2097168 | tf_op jit(solution)/shard_map/reduce_scatter | solution.py:203
  3257.4 713.0 %reduce-scatter.16.cloned.1.call-done = f32[64,8192]{1,0:T(8,128)} async-done(((f32[2048,8192]{1,0:T(8,128)}), f32[64,8192]{1,0:T(8,128)}) %reduce-scatter.16.cloned.1.call-update) | async-done | bytes 2097168 | tf_op jit(solution)/shard_map/reduce_scatter | solution.py:198
  (287 shorter events, 541.6 us)
Async XLA Ops:
  7.2 81.7 %all-gather.8.cloned.1.call-start = ((), (), s32[]{:S(2)}) async-start(), calls=%async_computation.15 | async-start | bytes 8650752 | tf_op jit(solution)/shard_map/all_gather | solution.py:105
  7.9 175.5 %all-gather.12.cloned.1.call-start = ((), (), s32[]{:S(2)}) async-start(), calls=%async_computation.17 | async-start | bytes 8650752 | tf_op jit(solution)/shard_map/all_gather | solution.py:104
  8.7 253.7 %all-gather.10.cloned.1.call-start = ((), (), s32[]{:S(2)}) async-start(), calls=%async_computation.16 | async-start | bytes 8650752 | tf_op jit(solution)/shard_map/all_gather | solution.py:103
  9.4 503.7 %all-gather.14.cloned.1.call-start = ((), (), s32[]{:S(2)}) async-start(), calls=%async_computation.18 | async-start | bytes 8650752 | tf_op jit(solution)/shard_map/all_gather | solution.py:106
  10.0 566.6 %all-gather.18.cloned.1.call-start = ((), (), s32[]{:S(2)}) async-start(), calls=%async_computation.20 | async-start | bytes 34603008 | tf_op jit(solution)/shard_map/all_gather | solution.py:163
  10.6 766.2 %all-gather.16.cloned.1.call-start = ((), (), s32[]{:S(2)}) async-start(), calls=%async_computation.19 | async-start | bytes 34603008 | tf_op jit(solution)/shard_map/all_gather | solution.py:162
  11.2 961.5 %all-gather.20.cloned.1.call-start = ((), (), s32[]{:S(2)}) async-start(), calls=%async_computation.21 | async-start | bytes 34603008 | tf_op jit(solution)/shard_map/all_gather | solution.py:164
  53.0 209.3 %copy-start.38 = (f32[2048]{0:T(1024)}, f32[2048]{0:T(1024)S(1)}, u32[]{:S(2)}) copy-start(f32[2048]{0:T(1024)S(1)} %convert_element_type.262) | copy-start | bytes 24580
  60.8 201.5 %copy-start.43 = (f32[256]{0:T(256)}, f32[256]{0:T(256)S(1)}, u32[]{:S(2)}) copy-start(f32[256]{0:T(256)S(1)} %add_rsqrt_fusion.1) | copy-start | bytes 3076
  112.2 194.4 %all-to-all-start = ((bf16[4,2,65536]{2,1,0:T(2,128)(2,1)}), bf16[4,2,65536]{2,1,0:T(2,128)(2,1)}, u32[]{:S(2)}, u32[]{:S(2)}) async-start(bf16[4,2,65536]{2,1,0:T(2,128)(2,1)} %reshape.873), calls=%async_computation | async-start | bytes 2097152 | tf_op jit(solution)/shard_map/all_to_all | solution.py:124
  306.6 49.2 %all-to-all-start.2 = ((bf16[4,2,65536]{2,1,0:T(2,128)(2,1)}), bf16[4,2,65536]{2,1,0:T(2,128)(2,1)S(1)}, u32[]{:S(2)}, u32[]{:S(2)}) async-start(bf16[4,2,65536]{2,1,0:T(2,128)(2,1)} %reshape.875), calls=%async_computation.2 | async-start | bytes 2097152 | tf_op jit(solution)/shard_map/all_to_all | solution.py:123
  355.8 46.7 %all-to-all-start.1 = ((bf16[4,2,65536]{2,1,0:T(2,128)(2,1)}), bf16[4,2,65536]{2,1,0:T(2,128)(2,1)}, u32[]{:S(2)}, u32[]{:S(2)}) async-start(bf16[4,2,65536]{2,1,0:T(2,128)(2,1)} %reshape.877), calls=%async_computation.1 | async-start | bytes 2097152 | tf_op jit(solution)/shard_map/all_to_all | solution.py:122
  456.3 51.8 %all-to-all-start.3 = ((bf16[4,2,65536]{2,1,0:T(2,128)(2,1)}), bf16[4,2,65536]{2,1,0:T(2,128)(2,1)S(1)}, u32[]{:S(2)}, u32[]{:S(2)}) async-start(bf16[4,2,65536]{2,1,0:T(2,128)(2,1)} %reshape.879), calls=%async_computation.3 | async-start | bytes 2097152 | tf_op jit(solution)/shard_map/all_to_all | solution.py:156
  463.2 1081.2 %reduce-scatter.14.cloned.1.call-start = ((), (), s32[]{:S(2)}) async-start(), calls=%async_computation.25 | async-start | bytes 17301504 | tf_op jit(solution)/shard_map/reduce_scatter | solution.py:298
  520.5 256.3 %copy-start.17 = (bf16[256,2048]{1,0:T(8,128)(2,1)}, bf16[256,2048]{1,0:T(8,128)(2,1)S(1)}, u32[]{:S(2)}) copy-start(bf16[256,2048]{1,0:T(8,128)(2,1)S(1)} %multiply_convert_fusion.5) | copy-start | bytes 3145732
  1064.6 34.8 all-to-all-start.4
  1070.5 473.8 %reduce-scatter.12.cloned.1.call-start = ((), (), s32[]{:S(2)}) async-start(), calls=%async_computation.24 | async-start | bytes 17301504 | tf_op jit(solution)/shard_map/reduce_scatter | solution.py:295
  1256.8 36.9 all-to-all-start.5
  1293.7 39.7 all-to-all-start.6
  1305.2 339.9 %reduce-scatter.8.cloned.1.call-start = ((), (), s32[]{:S(2)}) async-start(), calls=%async_computation.22 | async-start | bytes 17301504 | tf_op jit(solution)/shard_map/reduce_scatter | solution.py:289
  1358.5 474.0 %reduce-scatter.10.cloned.1.call-start = ((), (), s32[]{:S(2)}) async-start(), calls=%async_computation.23 | async-start | bytes 17301504 | tf_op jit(solution)/shard_map/reduce_scatter | solution.py:292
  1366.9 1177.3 %reduce-scatter.20.cloned.1.call-start = ((), (), s32[]{:S(2)}) async-start(), calls=%async_computation.28 | async-start | bytes 69206016 | tf_op jit(solution)/shard_map/reduce_scatter | solution.py:178
  1394.3 1863.1 %reduce-scatter.18.cloned.1.call-start = ((), (), s32[]{:S(2)}) async-start(), calls=%async_computation.27 | async-start | bytes 69206016 | tf_op jit(solution)/shard_map/reduce_scatter | solution.py:203
  1421.8 2548.5 %reduce-scatter.16.cloned.1.call-start = ((), (), s32[]{:S(2)}) async-start(), calls=%async_computation.26 | async-start | bytes 69206016 | tf_op jit(solution)/shard_map/reduce_scatter | solution.py:198
  (52 other events, 411.3 us)
Sparse Core Ops, SparseCore 0:
  10.9 77.9 all-gather.7
  91.7 91.6 all-gather.11
  186.3 76.0 all-gather.9
  265.1 91.3 all-gather.13
  359.2 217.3 all-gather.17
  579.3 197.4 all-gather.15
  779.7 192.9 all-gather.19
  1041.3 203.7 reduce-scatter.13
  1247.9 209.0 reduce-scatter.11
  1459.7 185.4 reduce-scatter.7
  1648.0 184.4 reduce-scatter.9
  1835.3 708.8 reduce-scatter.19
  2547.1 710.2 reduce-scatter.17
  3260.2 710.1 reduce-scatter.15
where the time goes:
time: 3990 us; the launch traced here: 3980 us
  waiting for transfers between devices  3160 us (79%)
  matrix products  322 us (8%)
  blocking collectives  152 us (4%)
  local copies, waits for them, and re-layouts  146 us (4%)
  other arithmetic  134 us (3%)
  starting transfers between devices  50.6 us (1%)
    reduce_scatter x1, waiting for transfers between devices, local(): lax.psum_scatter(outer_sum(normed_two, grad_up), ('seq', 'fsdp'), scatter...  713 us
    reduce_scatter x1, waiting for transfers between devices, local(): lax.psum_scatter(outer_sum(normed_two, grad_gate), ('seq', 'fsdp'), scatt...  713 us
    reduce_scatter x1, waiting for transfers between devices, local(): lax.psum_scatter(outer_sum(hidden, grad_outb), ('seq', 'fsdp'), scatter_d...  712 us
    reduce_scatter x1, waiting for transfers between devices, local(): lax.psum_scatter(outer_sum(normed_one, grad_key), ('seq', 'fsdp'), scatte...  187 us
    all_gather x1, waiting for transfers between devices, local(): lax.all_gather(w_gate, ('seq', 'fsdp'), axis=0, tiled=True)  183 us
    all_gather x1, waiting for transfers between devices, local(): lax.all_gather(w_down, ('seq', 'fsdp'), axis=0, tiled=True)  179 us
    dot_general x7, matrix products, outer_sum(): lax.dot_general(left, right, (((0,), (0,)), ((), ())), preferred_element_...  112 us
    reduce_scatter x1, waiting for transfers between devices, local(): lax.psum_scatter(outer_sum(normed_one, grad_query), ('seq', 'fsdp'), scat...  101 us
  transfers between devices with their start and end apart: 21, of which 17 were waited for; matrix products, arithmetic and copies ran while one was open for 13% of the time, Pallas kernels for 0%

commit v1 on v0

--- a/solution.py
+++ b/solution.py
@@ -9,6 +9,18 @@
 EPS = 1e-05
 ROPE_BASE = 130000.0
 NEG_FILL = -1e30
+
+
+def collect(x, axis, dim):
+    ways, here = (lax.axis_size(axis), lax.axis_index(axis))
+    grown, reach = (x, 1)
+    while reach < ways:
+        theirs = lax.ppermute(grown, axis, [(d, d ^ reach) for d in range(ways)])
+        mine_first = jnp.concatenate([grown, theirs], axis=dim)
+        theirs_first = jnp.concatenate([theirs, grown], axis=dim)
+        grown = jnp.where(here & reach == 0, mine_first, theirs_first)
+        reach = 2 * reach
+    return grown
 
 
 def tables(positions):
@@ -159,7 +171,7 @@
     mid_stream = residual_in + matmul(attended_tok, output_w)
     gain_two, gate_w, up_w, down_w = (
         lax.all_gather(norm2_gain, ("seq", "fsdp"), axis=0, tiled=True),
-        lax.all_gather(w_gate, ("seq", "fsdp"), axis=0, tiled=True),
+        collect(w_gate, ("seq", "fsdp"), 0),
         lax.all_gather(w_up, ("seq", "fsdp"), axis=0, tiled=True),
         lax.all_gather(w_down, ("seq", "fsdp"), axis=0, tiled=True),
     )

time: 3990 us -> 4900 us (1.23)
  waiting for transfers between devices: 3160 us -> 3740 us
  blocking collectives: 152 us -> 400 us
    all_to_all x1, waiting for transfers between devices: 20.6 us -> 683 us  [local(): lax.all_to_all(query_rot, 'seq', split_axis=2, concat_axis=1, tiled=True)]
    all_to_all x1, waiting for transfers between devices: 28.2 us -> 364 us  [local(): lax.all_to_all(key_rot, 'seq', split_axis=2, concat_axis=1, tiled=True)]
    unnamed x2, blocking collectives: 94.2 us -> 353 us
    reduce_scatter x1, waiting for transfers between devices: 0.01 us -> 187 us  [local(): lax.psum_scatter(outer_sum(normed_one, grad_value), ('seq', 'fsdp'), scat...]
    all_gather x1, waiting for transfers between devices: 183 us -> 0.01 us  [local(): lax.all_gather(w_gate, ('seq', 'fsdp'), axis=0, tiled=True)]
    all_gather x1, waiting for transfers between devices: 179 us -> 0.02 us  [local(): lax.all_gather(w_down, ('seq', 'fsdp'), axis=0, tiled=True)]
    ppermute x0 -> x5, waiting for transfers between devices: none -> 176 us  [collect(): theirs = lax.ppermute(grown, axis, [(d, d ^ reach) for d in range(ways)])]
    reduce_scatter x1, waiting for transfers between devices: 101 us -> 0.01 us  [local(): lax.psum_scatter(outer_sum(normed_one, grad_query), ('seq', 'fsdp'), scat...]
  transfers between devices with their start and end apart: 21 -> 26, of which waited for: 17 -> 13; matrix products, arithmetic and copies ran while one was open for 13% -> 12% of each run, Pallas kernels for 0% -> 0%
where the time goes in v1:
time: 4900 us; the launch traced here: 4890 us
  waiting for transfers between devices  3740 us (76%)
  blocking collectives  400 us (8%)
  matrix products  339 us (7%)
  other arithmetic  176 us (4%)
  local copies, waits for them, and re-layouts  152 us (3%)
  starting transfers between devices  67.3 us (1%)
    reduce_scatter x1, waiting for transfers between devices, local(): lax.psum_scatter(outer_sum(normed_two, grad_up), ('seq', 'fsdp'), scatter...  713 us
    reduce_scatter x1, waiting for transfers between devices, local(): lax.psum_scatter(outer_sum(hidden, grad_outb), ('seq', 'fsdp'), scatter_d...  713 us
    reduce_scatter x1, waiting for transfers between devices, local(): lax.psum_scatter(outer_sum(normed_two, grad_gate), ('seq', 'fsdp'), scatt...  712 us
    all_to_all x1, waiting for transfers between devices, local(): lax.all_to_all(query_rot, 'seq', split_axis=2, concat_axis=1, tiled=True)  683 us
    all_to_all x1, waiting for transfers between devices, local(): lax.all_to_all(key_rot, 'seq', split_axis=2, concat_axis=1, tiled=True)  364 us
    unnamed x2, blocking collectives  353 us
    reduce_scatter x1, waiting for transfers between devices, local(): lax.psum_scatter(outer_sum(normed_one, grad_value), ('seq', 'fsdp'), scat...  187 us
    ppermute x5, waiting for transfers between devices, collect(): theirs = lax.ppermute(grown, axis, [(d, d ^ reach) for d in range(ways)])  176 us
  transfers between devices with their start and end apart: 26, of which 13 were waited for; matrix products, arithmetic and copies ran while one was open for 12% of the time, Pallas kernels for 0%

profile of v1, /device:TPU:14, one launch (start us, length us, event | category | flops | bytes accessed | tf_op | source)
XLA Modules:
  0.0 4889.9 jit_solution(2343078704914833717)
XLA Ops:
  17.4 61.3 %collective-permute-done.1 = bf16[128,8192]{1,0:T(8,128)(2,1)} collective-permute-done((bf16[128,8192]{1,0:T(8,128)(2,1)S(1)}, bf16[128,8192]{1,0:T(8,128)(2,1)}, u32[]{:S(2)}, u32[]{:S(2)}) %collective-permute-start.1) | collective-permute-done | bytes 2097184 | tf_op jit(solution)/shard_map/ppermute | solution.py:18
  83.6 111.8 %collective-permute-done.2 = bf16[256,8192]{1,0:T(8,128)(2,1)} collective-permute-done((bf16[256,8192]{1,0:T(8,128)(2,1)}, bf16[256,8192]{1,0:T(8,128)(2,1)}, u32[]{:S(2)}, u32[]{:S(2)}) %collective-permute-start.2) | collective-permute-done | bytes 4194336 | tf_op jit(solution)/shard_map/ppermute | solution.py:18
  207.1 310.3 %all-reduce.7 = (bf16[2048]{0:T(1024)(128)(2,1)S(1)}, bf16[2048]{0:T(1024)(128)(2,1)S(1)}) all-reduce(bf16[2048]{0:T(1024)(128)(2,1)S(1)} %dynamic-update-slice.10, bf16[2048]{0:T(1024)(128)(2,1)S(1)} %dynamic-update-slice.11), channel_id=1, replica_groups=mesh['seq'=4,'fsdp'=8] {'seq','fsdp'}, use_global_device_ids=true, to_apply=%add.2 | all-reduce | flops 4096 | bytes 16384
  623.6 20.5 maximum_select_fusion.2
  666.2 364.0 %all-to-all-done.2 = bf16[4,2,65536]{2,1,0:T(2,128)(2,1)} async-done(((bf16[4,2,65536]{2,1,0:T(2,128)(2,1)}), bf16[4,2,65536]{2,1,0:T(2,128)(2,1)}, u32[]{:S(2)}, u32[]{:S(2)}) %all-to-all-start.2) | async-done | bytes 1048608 | tf_op jit(solution)/shard_map/all_to_all | solution.py:135
  1055.0 682.8 %all-to-all-done.1 = bf16[4,2,65536]{2,1,0:T(2,128)(2,1)} async-done(((bf16[4,2,65536]{2,1,0:T(2,128)(2,1)}), bf16[4,2,65536]{2,1,0:T(2,128)(2,1)}, u32[]{:S(2)}, u32[]{:S(2)}) %all-to-all-start.1) | async-done | bytes 1048608 | tf_op jit(solution)/shard_map/all_to_all | solution.py:134
  1798.0 23.0 all-to-all-done.3
  1833.8 19.3 fusion.61
  1853.2 17.0 fusion.86
  1870.2 33.4 multiply_convert_fusion.2
  1919.0 16.6 multiply_reduce_fusion.2
  1973.1 28.2 all-to-all-done.4
  2128.3 23.0 all-to-all-done.5
  2216.5 47.3 all_to_all.108
  2278.7 26.3 fusion.89
  2305.1 26.2 fusion.90
  2332.6 26.1 fusion.59
  2360.3 17.7 fusion.29
  2396.7 42.5 all-reduce.6
  2443.9 113.9 %reduce-scatter.10.cloned.1.call-done = f32[64,2048]{1,0:T(8,128)} async-done(((f32[2048,2048]{1,0:T(8,128)}), f32[64,2048]{1,0:T(8,128)}) %reduce-scatter.10.cloned.1.call-update) | async-done | bytes 524304 | tf_op jit(solution)/shard_map/reduce_scatter | solution.py:304
  2557.8 187.4 %reduce-scatter.12.cloned.1.call-done = f32[64,2048]{1,0:T(8,128)} async-done(((f32[2048,2048]{1,0:T(8,128)}), f32[64,2048]{1,0:T(8,128)}) %reduce-scatter.12.cloned.1.call-update) | async-done | bytes 524304 | tf_op jit(solution)/shard_map/reduce_scatter | solution.py:307
  2745.3 711.6 %reduce-scatter.16.cloned.1.call-done = f32[64,8192]{1,0:T(8,128)} async-done(((f32[2048,8192]{1,0:T(8,128)}), f32[64,8192]{1,0:T(8,128)}) %reduce-scatter.16.cloned.1.call-update) | async-done | bytes 2097168 | tf_op jit(solution)/shard_map/reduce_scatter | solution.py:210
  3456.8 713.2 %reduce-scatter.18.cloned.1.call-done = f32[64,8192]{1,0:T(8,128)} async-done(((f32[2048,8192]{1,0:T(8,128)}), f32[64,8192]{1,0:T(8,128)}) %reduce-scatter.18.cloned.1.call-update) | async-done | bytes 2097168 | tf_op jit(solution)/shard_map/reduce_scatter | solution.py:215
  4170.1 713.1 %reduce-scatter.20.cloned.1.call-done = f32[256,2048]{1,0:T(8,128)} async-done(((f32[8192,2048]{1,0:T(8,128)}), f32[256,2048]{1,0:T(8,128)}) %reduce-scatter.20.cloned.1.call-update) | async-done | bytes 2097168 | tf_op jit(solution)/shard_map/reduce_scatter | solution.py:190
  (326 shorter events, 538.0 us)
Async XLA Ops:
  7.2 518.8 %all-gather.8.cloned.1.call-start = ((), (), s32[]{:S(2)}) async-start(), calls=%async_computation.15 | async-start | bytes 8650752 | tf_op jit(solution)/shard_map/all_gather | solution.py:117
  7.9 553.0 %all-gather.10.cloned.1.call-start = ((), (), s32[]{:S(2)}) async-start(), calls=%async_computation.16 | async-start | bytes 8650752 | tf_op jit(solution)/shard_map/all_gather | solution.py:115
  8.7 562.3 %all-gather.12.cloned.1.call-start = ((), (), s32[]{:S(2)}) async-start(), calls=%async_computation.17 | async-start | bytes 8650752 | tf_op jit(solution)/shard_map/all_gather | solution.py:116
  9.4 1817.9 %all-gather.14.cloned.1.call-start = ((), (), s32[]{:S(2)}) async-start(), calls=%async_computation.18 | async-start | bytes 8650752 | tf_op jit(solution)/shard_map/all_gather | solution.py:118
  10.0 1823.8 %all-gather.18.cloned.1.call-start = ((), (), s32[]{:S(2)}) async-start(), calls=%async_computation.20 | async-start | bytes 34603008 | tf_op jit(solution)/shard_map/all_gather | solution.py:176
  10.6 1842.6 %all-gather.16.cloned.1.call-start = ((), (), s32[]{:S(2)}) async-start(), calls=%async_computation.19 | async-start | bytes 34603008 | tf_op jit(solution)/shard_map/all_gather | solution.py:175
  11.1 1892.5 %all-gather.20.cloned.1.call-start = ((), (), s32[]{:S(2)}) async-start(), calls=%async_computation.21 | async-start | bytes 34603008 | tf_op jit(solution)/shard_map/all_gather | solution.py:195
  16.8 61.9 %collective-permute-start.1 = (bf16[128,8192]{1,0:T(8,128)(2,1)S(1)}, bf16[128,8192]{1,0:T(8,128)(2,1)}, u32[]{:S(2)}, u32[]{:S(2)}) collective-permute-start(bf16[128,8192]{1,0:T(8,128)(2,1)S(1)} %maximum_select_fusion.5), channel_id=1, source_target_pairs={{0,2},{1,3},{2,0},{3,1},{4,6},{5,7},{6,4},{7,5},{8,10},{9,11},{10,... | collective-permute-start | bytes 6291464 | tf_op jit(solution)/shard_map/ppermute | solution.py:18
  83.1 112.2 %collective-permute-start.2 = (bf16[256,8192]{1,0:T(8,128)(2,1)}, bf16[256,8192]{1,0:T(8,128)(2,1)}, u32[]{:S(2)}, u32[]{:S(2)}) collective-permute-start(bf16[256,8192]{1,0:T(8,128)(2,1)} %maximum_select_fusion.4), channel_id=1, source_target_pairs={{0,4},{1,5},{2,6},{3,7},{4,0},{5,1},{6,2},{7,3},{8,12},{9,13},{10,... | collective-permute-start | bytes 12582920 | tf_op jit(solution)/shard_map/ppermute | solution.py:18
  206.2 417.4 %collective-permute-start.3 = (bf16[512,8192]{1,0:T(8,128)(2,1)}, bf16[512,8192]{1,0:T(8,128)(2,1)}, u32[]{:S(2)}, u32[]{:S(2)}) collective-permute-start(bf16[512,8192]{1,0:T(8,128)(2,1)} %maximum_select_fusion.3), channel_id=1, source_target_pairs={{0,8},{1,9},{2,10},{3,11},{4,12},{5,13},{6,14},{7,15},{8,0},{9,1},... | collective-permute-start | bytes 25165832 | tf_op jit(solution)/shard_map/ppermute | solution.py:18
  555.2 63.3 %all-to-all-start = ((bf16[4,2,65536]{2,1,0:T(2,128)(2,1)}), bf16[4,2,65536]{2,1,0:T(2,128)(2,1)}, u32[]{:S(2)}, u32[]{:S(2)}) async-start(bf16[4,2,65536]{2,1,0:T(2,128)(2,1)} %reshape.873), calls=%async_computation | async-start | bytes 2097152 | tf_op jit(solution)/shard_map/all_to_all | solution.py:136
  618.5 411.7 %all-to-all-start.2 = ((bf16[4,2,65536]{2,1,0:T(2,128)(2,1)}), bf16[4,2,65536]{2,1,0:T(2,128)(2,1)}, u32[]{:S(2)}, u32[]{:S(2)}) async-start(bf16[4,2,65536]{2,1,0:T(2,128)(2,1)} %reshape.875), calls=%async_computation.2 | async-start | bytes 2097152 | tf_op jit(solution)/shard_map/all_to_all | solution.py:135
  644.1 1226.1 %collective-permute-start.4 = (bf16[1024,8192]{1,0:T(8,128)(2,1)}, bf16[1024,8192]{1,0:T(8,128)(2,1)}, u32[]{:S(2)}, u32[]{:S(2)}) collective-permute-start(bf16[1024,8192]{1,0:T(8,128)(2,1)} %maximum_select_fusion.2), channel_id=1, source_target_pairs={{0,16},{1,17},{2,18},{3,19},{4,20},{5,21},{6,22},{7,23},{8,24},{9,... | collective-permute-start | bytes 50331656 | tf_op jit(solution)/shard_map/ppermute | solution.py:18
  1030.3 707.6 %all-to-all-start.1 = ((bf16[4,2,65536]{2,1,0:T(2,128)(2,1)}), bf16[4,2,65536]{2,1,0:T(2,128)(2,1)}, u32[]{:S(2)}, u32[]{:S(2)}) async-start(bf16[4,2,65536]{2,1,0:T(2,128)(2,1)} %reshape.877), calls=%async_computation.1 | async-start | bytes 2097152 | tf_op jit(solution)/shard_map/all_to_all | solution.py:134
  1798.0 645.8 %reduce-scatter.14.cloned.1.call-start = ((), (), s32[]{:S(2)}) async-start(), calls=%async_computation.25 | async-start | bytes 17301504 | tf_op jit(solution)/shard_map/reduce_scatter | solution.py:310
  1966.0 35.3 all-to-all-start.4
  2062.0 48.1 all-to-all-start.6
  2110.1 41.3 all-to-all-start.5
  2123.3 320.6 %reduce-scatter.8.cloned.1.call-start = ((), (), s32[]{:S(2)}) async-start(), calls=%async_computation.22 | async-start | bytes 17301504 | tf_op jit(solution)/shard_map/reduce_scatter | solution.py:301
  2176.7 381.2 %reduce-scatter.10.cloned.1.call-start = ((), (), s32[]{:S(2)}) async-start(), calls=%async_computation.23 | async-start | bytes 17301504 | tf_op jit(solution)/shard_map/reduce_scatter | solution.py:304
  2186.3 558.9 %reduce-scatter.12.cloned.1.call-start = ((), (), s32[]{:S(2)}) async-start(), calls=%async_computation.24 | async-start | bytes 17301504 | tf_op jit(solution)/shard_map/reduce_scatter | solution.py:307
  2277.5 1179.3 %reduce-scatter.16.cloned.1.call-start = ((), (), s32[]{:S(2)}) async-start(), calls=%async_computation.26 | async-start | bytes 69206016 | tf_op jit(solution)/shard_map/reduce_scatter | solution.py:210
  2305.1 1865.0 %reduce-scatter.18.cloned.1.call-start = ((), (), s32[]{:S(2)}) async-start(), calls=%async_computation.27 | async-start | bytes 69206016 | tf_op jit(solution)/shard_map/reduce_scatter | solution.py:215
  2331.3 2551.8 %reduce-scatter.20.cloned.1.call-start = ((), (), s32[]{:S(2)}) async-start(), calls=%async_computation.28 | async-start | bytes 69206016 | tf_op jit(solution)/shard_map/reduce_scatter | solution.py:190
  (69 other events, 1779.8 us)
Sparse Core Ops, SparseCore 0:
  10.9 91.0 all-gather.7
  104.8 94.4 all-gather.9
  202.2 107.5 all-gather.11
  312.5 108.8 all-gather.13
  424.1 634.7 all-gather.17
  1061.5 269.5 all-gather.15
  1334.0 269.4 all-gather.19
  1946.3 210.5 reduce-scatter.13
  2176.8 191.8 reduce-scatter.7
  2371.4 186.3 reduce-scatter.9
  2560.7 184.5 reduce-scatter.11
  2748.0 708.7 reduce-scatter.15
  3459.8 710.2 reduce-scatter.17
  4172.8 710.2 reduce-scatter.19
